TPU v7x, 1024 devices: a whole 4x4x32 slice. The times are simulated.
1024 devices in a mesh: ctx: 128 (over x_hi, z, core), tp: 8 (over x_lo, y).
Axes of the slice: x: 4 (x_hi: 2, x_lo: 2; x = x_hi * 2 + x_lo), y: 4, z: 32, core: 2. Of those that a mesh axis runs over, the one named last changes fastest.
Arguments:
- queries: bfloat16 [49152, 16, 128], P('ctx', 'tp'), may hold values from -6 to 6
- key_tensor: bfloat16 [49152, 2, 128], P('ctx'), may hold values from -6 to 6
- value_tensor: bfloat16 [49152, 2, 128], P('ctx'), may hold values from -6 to 6
- attn_output: bfloat16 [49152, 16, 128], P('ctx', 'tp'), may hold values from -4 to 4
- logsumexp_rows: float32 [16, 49152], P('tp', 'ctx'), may hold values from 4 to 7
- grad_output: bfloat16 [49152, 8192], P(('ctx', 'tp')), may hold values from -6 to 6
- out_proj: bfloat16 [2048, 8192], P('tp'), may hold values from -0.0625 to 0.0625
- block_doc: int32 [384], replicated, may hold values from 0 to 95, never falling along the last dimension, each value on 1 to 12 neighbouring positions
Outputs:
- grad_query: bfloat16 [49152, 16, 128], P('ctx', 'tp')
- grad_key: bfloat16 [49152, 2, 128], P(('ctx', 'tp'))
- grad_value: bfloat16 [49152, 2, 128], P(('ctx', 'tp'))
Inputs may be any that keep to these rules, and one draw needn't show every extreme that they name: `block_doc`: document ids never fall along the sequence; one document spans 1 to 12 blocks, and some document spans exactly 12 in every draw.
All inputs are finite; a program needn't handle non-finite values.
Results may differ from a plain program's by a relative error of at most 0.012.
Values may be sent and summed in bfloat16 or wider, within the bound.
A program may use at most 32 MiB of HBM per device.

v0:
```python
import jax
import jax.numpy as jnp
from jax import lax
from jax.sharding import PartitionSpec as P

QUERY_HEADS = 16
KEY_VALUE_HEADS = 2
DOCBLK = 128
RANKS_BACK = 4


def passed_along(shard, axis, by):
    peers = lax.axis_size(axis)
    pairs = [(i, i + by) for i in range(peers) if 0 <= i + by < peers]
    return lax.ppermute(shard, axis, pairs)


def from_behind(block, axis, distance):
    devices = range(lax.axis_size(axis))
    route = [((i - distance) % len(devices), i) for i in devices]
    return lax.ppermute(block, axis, route)


def doc_labels(block_doc, source_rank, row_count, block_size):
    block_count = row_count // block_size
    labels = lax.dynamic_slice_in_dim(block_doc, source_rank * block_count, block_count)
    return jnp.repeat(labels, block_size, total_repeat_length=row_count)


def tile_terms(
    allowed,
    query_block,
    gradient_block,
    logsumexp_block,
    delta_block,
    key_blk,
    value_blk,
    score_scale,
):
    scores = (
        jnp.einsum("ihd,jd->hij", query_block, key_blk, preferred_element_type=jnp.float32)
        * score_scale
    )
    prob_full = jnp.exp(jnp.where(allowed[None], scores - logsumexp_block[:, :, None], -1e30))
    dprobs = jnp.einsum(
        "ihd,jd->hij", gradient_block, value_blk, preferred_element_type=jnp.float32
    )
    dscores = (prob_full * (dprobs - delta_block[:, :, None]) * score_scale).astype(jnp.bfloat16)
    grad_q_part = jnp.einsum("hij,jd->ihd", dscores, key_blk, preferred_element_type=jnp.float32)
    grad_k_part = jnp.einsum(
        "hij,ihd->jd", dscores, query_block, preferred_element_type=jnp.float32
    )
    grad_v_part = jnp.einsum(
        "hij,ihd->jd",
        prob_full.astype(jnp.bfloat16),
        gradient_block,
        preferred_element_type=jnp.float32,
    )
    return (grad_q_part, grad_k_part, grad_v_part)


def per_device(
    queries, key_tensor, value_tensor, attn_output, logsumexp_rows, grad_output, out_proj, block_doc
):
    row_count = queries.shape[0]
    window_heads = queries.shape[1]
    head_dim = queries.shape[2]
    kv_heads = key_tensor.shape[1]
    cycle_size = lax.axis_size("ctx")
    span_ranks = min(RANKS_BACK, cycle_size // 2)
    score_scale = head_dim ** (-0.5)
    my_rank = lax.axis_index("ctx")
    group_number_index = lax.axis_index("tp") * window_heads // (QUERY_HEADS // KEY_VALUE_HEADS)
    offsets = jnp.arange(row_count, dtype=jnp.int32)
    product = lax.dot_general(
        lax.all_gather(grad_output, "tp", axis=0, tiled=True),
        out_proj,
        (((1,), (1,)), ((), ())),
        preferred_element_type=jnp.float32,
    )
    head_gradients = product.astype(jnp.bfloat16)
    head_gradients = head_gradients.reshape(row_count, window_heads, head_dim)
    delta_terms = jnp.sum(
        head_gradients.astype(jnp.float32) * attn_output.astype(jnp.float32), axis=2
    ).T
    key_mine = lax.dynamic_index_in_dim(key_tensor, group_number_index, 1, keepdims=False)
    value_mine = lax.dynamic_index_in_dim(value_tensor, group_number_index, 1, keepdims=False)

    def pair_terms(
        query_block,
        gradient_block,
        logsumexp_block,
        delta_block,
        query_rank,
        key_blk,
        value_blk,
        key_rank,
    ):
        query_pos = query_rank * row_count + offsets
        key_pos = key_rank * row_count + offsets
        query_doc = doc_labels(block_doc, query_rank, row_count, DOCBLK)
        key_doc = doc_labels(block_doc, key_rank, row_count, DOCBLK)
        allowed = (query_doc[:, None] == key_doc[None, :]) & (
            key_pos[None, :] <= query_pos[:, None]
        )
        return tile_terms(
            allowed,
            query_block,
            gradient_block,
            logsumexp_block,
            delta_block,
            key_blk,
            value_blk,
            score_scale,
        )

    first_q, first_k, first_v = pair_terms(
        queries, head_gradients, logsumexp_rows, delta_terms, my_rank, key_mine, value_mine, my_rank
    )

    def query_turn(cycle_step, carry):
        query_move, grad_move, sums_move, delta_move, query_acc, key_acc, value_acc = carry
        query_move, grad_move = passed_along((query_move, grad_move), "ctx", -1)
        sums_move, delta_move, query_acc = from_behind(
            (sums_move, delta_move, query_acc), "ctx", -1
        )
        source_rank = (my_rank + cycle_step) % cycle_size
        part_q, part_k, part_v = pair_terms(
            query_move, grad_move, sums_move, delta_move, source_rank, key_mine, value_mine, my_rank
        )
        return (
            query_move,
            grad_move,
            sums_move,
            delta_move,
            query_acc + part_q,
            key_acc + part_k,
            value_acc + part_v,
        )

    start_state = (queries, head_gradients, logsumexp_rows, delta_terms, first_q, first_k, first_v)
    final_state = lax.fori_loop(1, span_ranks + 1, query_turn, start_state)
    query_total = from_behind(final_state[4].astype(jnp.bfloat16), "ctx", span_ranks).astype(
        jnp.float32
    )
    key_total = final_state[5]
    value_total = final_state[6]
    head_mask = (jnp.arange(kv_heads, dtype=jnp.int32) == group_number_index).astype(jnp.float32)
    key_full = key_total[:, None, :] * head_mask[None, :, None]
    value_full = value_total[:, None, :] * head_mask[None, :, None]
    key_part, value_part = (
        lax.psum_scatter(
            key_full.astype(jnp.bfloat16), "tp", scatter_dimension=0, tiled=True
        ).astype(jnp.float32),
        lax.psum_scatter(
            value_full.astype(jnp.bfloat16), "tp", scatter_dimension=0, tiled=True
        ).astype(jnp.float32),
    )
    return (
        query_total.astype(jnp.bfloat16),
        key_part.astype(jnp.bfloat16),
        value_part.astype(jnp.bfloat16),
    )


def solution(mesh):
    placed = (
        P("ctx", "tp", None),
        P("ctx", None, None),
        P("ctx", None, None),
        P("ctx", "tp", None),
        P("tp", "ctx"),
        P(("ctx", "tp"), None),
        P("tp", None),
        P(),
    )
    return jax.shard_map(
        per_device,
        mesh=mesh,
        in_specs=placed,
        out_specs=(
            P("ctx", "tp", None),
            P(("ctx", "tp"), None, None),
            P(("ctx", "tp"), None, None),
        ),
        check_vma=False,
    )
```

profile of v0, /device:TPU:4, one launch (start us, length us, event | category | flops | bytes accessed | tf_op | source)
XLA Modules:
  0.0 314.5 jit_solution(4228581607888976061)
XLA Ops:
  10.4 2.0 select_select_fusion.2
  13.0 94.9 %all-gather.2.cloned.1.call-done = bf16[384,8192]{1,0:T(8,128)(2,1)} async-done(((bf16[48,8192]{1,0:T(8,128)(2,1)}), bf16[384,8192]{1,0:T(8,128)(2,1)}) %all-gather.2.cloned.1.call-update) | async-done | bytes 6291472 | tf_op jit(solution)/shard_map/all_gather | solution.py:76
  107.9 6.4 %convolution_convert_fusion = bf16[384,256]{0,1:T(8,128)(2,1)S(1)} fusion(bf16[384,8192]{1,0:T(8,128)(2,1)} %all-gather.2.cloned.1.call-done, bf16[256,8192]{1,0:T(8,128)(2,1)} %param.26), kind=kOutput, calls=%fused_computation.41 | convolution fusion | flops 1610711040 | bytes 10682368 | tf_op jit(solution)/shard_map/dot_general | solution.py:75
  116.7 89.7 %while.35 = (s32[]{:T(128)}, bf16[384,2,128]{2,0,1:T(8,128)(2,1)S(1)}, bf16[384,2,128]{2,0,1:T(8,128)(2,1)S(1)}, f32[2,384]{1,0:T(2,128)S(1)}, f32[2,384]{1,0:T(...) while((s32[]{:T(128)}, ...), condition=%wide.region_2.4_spmd.clone.clone, body=%wide.region_1.3_spmd.clone.clone.sunk | while | flops 380496384 | bytes 12245660 | solution.py:142
  116.7 7.0 %collective-permute-start.3 = (f32[2,384]{1,0:T(2,128)S(1)}, f32[2,384]{1,0:T(2,128)S(1)}, u32[]{:S(2)}, u32[]{:S(2)}) collective-permute-start(f32[2,384]{1,0:T(2,128)S(1)} %get-tuple-element.775), channel_id=1, source_target_pairs={{8,0},{16,8},{24,16},{32,24},{40,32},{48,40},{56,48},{64,56},{72,6... | collective-permute-start | bytes 9224 | tf_op jit(solution)/shard_map/while/body/eval_jaxpr/ppermute | solution.py:21
  123.7 2.8 collective-permute-start.2
  126.5 2.6 collective-permute-start.1
  129.0 2.8 collective-permute-start
  131.8 2.5 collective-permute-start.4
  135.7 1.9 select_select_fusion.4
  141.8 5.7 %collective-permute-start.3 = (f32[2,384]{1,0:T(2,128)S(1)}, f32[2,384]{1,0:T(2,128)S(1)}, u32[]{:S(2)}, u32[]{:S(2)}) collective-permute-start(f32[2,384]{1,0:T(2,128)S(1)} %get-tuple-element.775), channel_id=1, source_target_pairs={{8,0},{16,8},{24,16},{32,24},{40,32},{48,40},{56,48},{64,56},{72,6... | collective-permute-start | bytes 9224 | tf_op jit(solution)/shard_map/while/body/eval_jaxpr/ppermute | solution.py:21
  147.4 1.9 collective-permute-start.2
  151.3 2.3 collective-permute-start
  153.6 2.8 collective-permute-start.4
  157.8 1.9 select_select_fusion.4
  163.8 5.7 %collective-permute-start.3 = (f32[2,384]{1,0:T(2,128)S(1)}, f32[2,384]{1,0:T(2,128)S(1)}, u32[]{:S(2)}, u32[]{:S(2)}) collective-permute-start(f32[2,384]{1,0:T(2,128)S(1)} %get-tuple-element.775), channel_id=1, source_target_pairs={{8,0},{16,8},{24,16},{32,24},{40,32},{48,40},{56,48},{64,56},{72,6... | collective-permute-start | bytes 9224 | tf_op jit(solution)/shard_map/while/body/eval_jaxpr/ppermute | solution.py:21
  178.6 1.9 select_select_fusion.4
  184.6 6.0 %collective-permute-start.3 = (f32[2,384]{1,0:T(2,128)S(1)}, f32[2,384]{1,0:T(2,128)S(1)}, u32[]{:S(2)}, u32[]{:S(2)}) collective-permute-start(f32[2,384]{1,0:T(2,128)S(1)} %get-tuple-element.775), channel_id=1, source_target_pairs={{8,0},{16,8},{24,16},{32,24},{40,32},{48,40},{56,48},{64,56},{72,6... | collective-permute-start | bytes 9224 | tf_op jit(solution)/shard_map/while/body/eval_jaxpr/ppermute | solution.py:21
  194.5 2.5 collective-permute-start
  197.0 2.1 collective-permute-start.4
  200.4 1.9 select_select_fusion.4
  207.9 4.9 %collective-permute-start.5 = (bf16[384,2,128]{2,1,0:T(2,128)(2,1)S(1)}, bf16[384,2,128]{2,1,0:T(2,128)(2,1)S(1)}, u32[]{:S(2)}, u32[]{:S(2)}) collective-permute-start(bf16[384,2,128]{2,1,0:T(2,128)(2,1)S(1)} %copy.80), channel_id=1, source_target_pairs={{992,0},{1000,8},{1008,16},{1016,24},{0,32},{8,40},{16,48},{24,56}... | collective-permute-start | bytes 589832 | tf_op jit(solution)/shard_map/ppermute | solution.py:21
  214.7 10.5 %collective-permute-done.5 = bf16[384,2,128]{2,1,0:T(2,128)(2,1)S(1)} collective-permute-done((bf16[384,2,128]{2,1,0:T(2,128)(2,1)S(1)}, bf16[384,2,128]{2,1,0:T(2,128)(2,1)S(1)}, u32[]{:S(2)}, u32[]{:S(2)}) %collective-permute-start.5) | collective-permute-done | bytes 196640 | tf_op jit(solution)/shard_map/ppermute | solution.py:21
  225.2 79.0 %all-reduce.5.cloned.1.call-done = (bf16[384,2,128]{2,1,0:T(2,128)(2,1)}, bf16[384,2,128]{2,1,0:T(2,128)(2,1)}) async-done(((bf16[384,2,128]{2,1,0:T(2,128)(2,1)}, bf16[384,2,128]{2,1,0:T(2,128)(2,1)}), (bf16[384,2,128]{2,1,0:T(2,128)(2,1)}, bf16[384,2,128]{2,1,0:T(2,128)(2,1)})) %all-reduce.5.cloned.1.call-update) | async-done | bytes 393232
  (126 shorter events, 46.8 us)
Async XLA Ops:
  7.2 100.8 %all-gather.2.cloned.1.call-start = ((), (), s32[]{:S(2)}) async-start(), calls=%async_computation | async-start | bytes 7077888 | tf_op jit(solution)/shard_map/all_gather | solution.py:76
  8.0 296.2 %all-reduce.5.cloned.1.call-start = ((), (), s32[]{:S(2)}) async-start(), calls=%async_computation.1 | async-start | bytes 786432
  13.0 101.6 %copy-start.3 = (bf16[384,2,128]{2,1,0:T(2,128)(2,1)S(1)}, bf16[384,2,128]{2,1,0:T(2,128)(2,1)}, u32[]{:S(2)}) copy-start(bf16[384,2,128]{2,1,0:T(2,128)(2,1)} %param.23) | copy-start | bytes 589828
  116.7 23.1 %collective-permute-start.3 = (f32[2,384]{1,0:T(2,128)S(1)}, f32[2,384]{1,0:T(2,128)S(1)}, u32[]{:S(2)}, u32[]{:S(2)}) collective-permute-start(f32[2,384]{1,0:T(2,128)S(1)} %get-tuple-element.775), channel_id=1, source_target_pairs={{8,0},{16,8},{24,16},{32,24},{40,32},{48,40},{56,48},{64,56},{72,6... | collective-permute-start | bytes 9224 | tf_op jit(solution)/shard_map/while/body/eval_jaxpr/ppermute | solution.py:21
  123.7 16.1 %collective-permute-start.2 = (f32[2,384]{1,0:T(2,128)S(1)}, f32[2,384]{1,0:T(2,128)S(1)}, u32[]{:S(2)}, u32[]{:S(2)}) collective-permute-start(f32[2,384]{1,0:T(2,128)S(1)} %get-tuple-element.774), channel_id=1, source_target_pairs={{8,0},{16,8},{24,16},{32,24},{40,32},{48,40},{56,48},{64,56},{72,6... | collective-permute-start | bytes 9224 | tf_op jit(solution)/shard_map/while/body/eval_jaxpr/ppermute | solution.py:21
  126.5 13.8 %collective-permute-start.1 = (bf16[384,2,128]{2,0,1:T(8,128)(2,1)S(1)}, bf16[384,2,128]{2,0,1:T(8,128)(2,1)S(1)}, u32[]{:S(2)}, u32[]{:S(2)}) collective-permute-start(bf16[384,2,128]{2,0,1:T(8,128)(2,1)S(1)} %get-tuple-element.773), channel_id=1, source_target_pairs={{8,0},{16,8},{24,16},{32,24},{40,32},{48,40},{56,48},{64,56},{72,6... | collective-permute-start | bytes 589832 | tf_op jit(solution)/shard_map/while/body/eval_jaxpr/ppermute | solution.py:15
  129.0 10.8 %collective-permute-start = (bf16[384,2,128]{2,0,1:T(8,128)(2,1)S(1)}, bf16[384,2,128]{2,0,1:T(8,128)(2,1)S(1)}, u32[]{:S(2)}, u32[]{:S(2)}) collective-permute-start(bf16[384,2,128]{2,0,1:T(8,128)(2,1)S(1)} %get-tuple-element.772), channel_id=1, source_target_pairs={{8,0},{16,8},{24,16},{32,24},{40,32},{48,40},{56,48},{64,56},{72,6... | collective-permute-start | bytes 589832 | tf_op jit(solution)/shard_map/while/body/eval_jaxpr/ppermute | solution.py:15
  131.8 9.6 %collective-permute-start.4 = (f32[384,2,128]{2,0,1:T(8,128)S(1)}, f32[384,2,128]{2,0,1:T(8,128)S(1)}, u32[]{:S(2)}, u32[]{:S(2)}) collective-permute-start(f32[384,2,128]{2,0,1:T(8,128)S(1)} %get-tuple-element.776), channel_id=1, source_target_pairs={{8,0},{16,8},{24,16},{32,24},{40,32},{48,40},{56,48},{64,56},{72,6... | collective-permute-start | bytes 1179656 | tf_op jit(solution)/shard_map/while/body/eval_jaxpr/ppermute | solution.py:21
  141.8 20.1 %collective-permute-start.3 = (f32[2,384]{1,0:T(2,128)S(1)}, f32[2,384]{1,0:T(2,128)S(1)}, u32[]{:S(2)}, u32[]{:S(2)}) collective-permute-start(f32[2,384]{1,0:T(2,128)S(1)} %get-tuple-element.775), channel_id=1, source_target_pairs={{8,0},{16,8},{24,16},{32,24},{40,32},{48,40},{56,48},{64,56},{72,6... | collective-permute-start | bytes 9224 | tf_op jit(solution)/shard_map/while/body/eval_jaxpr/ppermute | solution.py:21
  147.4 14.4 %collective-permute-start.2 = (f32[2,384]{1,0:T(2,128)S(1)}, f32[2,384]{1,0:T(2,128)S(1)}, u32[]{:S(2)}, u32[]{:S(2)}) collective-permute-start(f32[2,384]{1,0:T(2,128)S(1)} %get-tuple-element.774), channel_id=1, source_target_pairs={{8,0},{16,8},{24,16},{32,24},{40,32},{48,40},{56,48},{64,56},{72,6... | collective-permute-start | bytes 9224 | tf_op jit(solution)/shard_map/while/body/eval_jaxpr/ppermute | solution.py:21
  149.4 13.0 %collective-permute-start.1 = (bf16[384,2,128]{2,0,1:T(8,128)(2,1)S(1)}, bf16[384,2,128]{2,0,1:T(8,128)(2,1)S(1)}, u32[]{:S(2)}, u32[]{:S(2)}) collective-permute-start(bf16[384,2,128]{2,0,1:T(8,128)(2,1)S(1)} %get-tuple-element.773), channel_id=1, source_target_pairs={{8,0},{16,8},{24,16},{32,24},{40,32},{48,40},{56,48},{64,56},{72,6... | collective-permute-start | bytes 589832 | tf_op jit(solution)/shard_map/while/body/eval_jaxpr/ppermute | solution.py:15
  151.3 10.6 %collective-permute-start = (bf16[384,2,128]{2,0,1:T(8,128)(2,1)S(1)}, bf16[384,2,128]{2,0,1:T(8,128)(2,1)S(1)}, u32[]{:S(2)}, u32[]{:S(2)}) collective-permute-start(bf16[384,2,128]{2,0,1:T(8,128)(2,1)S(1)} %get-tuple-element.772), channel_id=1, source_target_pairs={{8,0},{16,8},{24,16},{32,24},{40,32},{48,40},{56,48},{64,56},{72,6... | collective-permute-start | bytes 589832 | tf_op jit(solution)/shard_map/while/body/eval_jaxpr/ppermute | solution.py:15
  153.6 9.8 %collective-permute-start.4 = (f32[384,2,128]{2,0,1:T(8,128)S(1)}, f32[384,2,128]{2,0,1:T(8,128)S(1)}, u32[]{:S(2)}, u32[]{:S(2)}) collective-permute-start(f32[384,2,128]{2,0,1:T(8,128)S(1)} %get-tuple-element.776), channel_id=1, source_target_pairs={{8,0},{16,8},{24,16},{32,24},{40,32},{48,40},{56,48},{64,56},{72,6... | collective-permute-start | bytes 1179656 | tf_op jit(solution)/shard_map/while/body/eval_jaxpr/ppermute | solution.py:21
  163.8 18.9 %collective-permute-start.3 = (f32[2,384]{1,0:T(2,128)S(1)}, f32[2,384]{1,0:T(2,128)S(1)}, u32[]{:S(2)}, u32[]{:S(2)}) collective-permute-start(f32[2,384]{1,0:T(2,128)S(1)} %get-tuple-element.775), channel_id=1, source_target_pairs={{8,0},{16,8},{24,16},{32,24},{40,32},{48,40},{56,48},{64,56},{72,6... | collective-permute-start | bytes 9224 | tf_op jit(solution)/shard_map/while/body/eval_jaxpr/ppermute | solution.py:21
  169.5 13.2 %collective-permute-start.2 = (f32[2,384]{1,0:T(2,128)S(1)}, f32[2,384]{1,0:T(2,128)S(1)}, u32[]{:S(2)}, u32[]{:S(2)}) collective-permute-start(f32[2,384]{1,0:T(2,128)S(1)} %get-tuple-element.774), channel_id=1, source_target_pairs={{8,0},{16,8},{24,16},{32,24},{40,32},{48,40},{56,48},{64,56},{72,6... | collective-permute-start | bytes 9224 | tf_op jit(solution)/shard_map/while/body/eval_jaxpr/ppermute | solution.py:21
  171.4 11.7 %collective-permute-start.1 = (bf16[384,2,128]{2,0,1:T(8,128)(2,1)S(1)}, bf16[384,2,128]{2,0,1:T(8,128)(2,1)S(1)}, u32[]{:S(2)}, u32[]{:S(2)}) collective-permute-start(bf16[384,2,128]{2,0,1:T(8,128)(2,1)S(1)} %get-tuple-element.773), channel_id=1, source_target_pairs={{8,0},{16,8},{24,16},{32,24},{40,32},{48,40},{56,48},{64,56},{72,6... | collective-permute-start | bytes 589832 | tf_op jit(solution)/shard_map/while/body/eval_jaxpr/ppermute | solution.py:15
  173.3 9.3 %collective-permute-start = (bf16[384,2,128]{2,0,1:T(8,128)(2,1)S(1)}, bf16[384,2,128]{2,0,1:T(8,128)(2,1)S(1)}, u32[]{:S(2)}, u32[]{:S(2)}) collective-permute-start(bf16[384,2,128]{2,0,1:T(8,128)(2,1)S(1)} %get-tuple-element.772), channel_id=1, source_target_pairs={{8,0},{16,8},{24,16},{32,24},{40,32},{48,40},{56,48},{64,56},{72,6... | collective-permute-start | bytes 589832 | tf_op jit(solution)/shard_map/while/body/eval_jaxpr/ppermute | solution.py:15
  175.2 8.9 %collective-permute-start.4 = (f32[384,2,128]{2,0,1:T(8,128)S(1)}, f32[384,2,128]{2,0,1:T(8,128)S(1)}, u32[]{:S(2)}, u32[]{:S(2)}) collective-permute-start(f32[384,2,128]{2,0,1:T(8,128)S(1)} %get-tuple-element.776), channel_id=1, source_target_pairs={{8,0},{16,8},{24,16},{32,24},{40,32},{48,40},{56,48},{64,56},{72,6... | collective-permute-start | bytes 1179656 | tf_op jit(solution)/shard_map/while/body/eval_jaxpr/ppermute | solution.py:21
  184.6 19.9 %collective-permute-start.3 = (f32[2,384]{1,0:T(2,128)S(1)}, f32[2,384]{1,0:T(2,128)S(1)}, u32[]{:S(2)}, u32[]{:S(2)}) collective-permute-start(f32[2,384]{1,0:T(2,128)S(1)} %get-tuple-element.775), channel_id=1, source_target_pairs={{8,0},{16,8},{24,16},{32,24},{40,32},{48,40},{56,48},{64,56},{72,6... | collective-permute-start | bytes 9224 | tf_op jit(solution)/shard_map/while/body/eval_jaxpr/ppermute | solution.py:21
  190.6 13.9 %collective-permute-start.2 = (f32[2,384]{1,0:T(2,128)S(1)}, f32[2,384]{1,0:T(2,128)S(1)}, u32[]{:S(2)}, u32[]{:S(2)}) collective-permute-start(f32[2,384]{1,0:T(2,128)S(1)} %get-tuple-element.774), channel_id=1, source_target_pairs={{8,0},{16,8},{24,16},{32,24},{40,32},{48,40},{56,48},{64,56},{72,6... | collective-permute-start | bytes 9224 | tf_op jit(solution)/shard_map/while/body/eval_jaxpr/ppermute | solution.py:21
  192.6 12.4 %collective-permute-start.1 = (bf16[384,2,128]{2,0,1:T(8,128)(2,1)S(1)}, bf16[384,2,128]{2,0,1:T(8,128)(2,1)S(1)}, u32[]{:S(2)}, u32[]{:S(2)}) collective-permute-start(bf16[384,2,128]{2,0,1:T(8,128)(2,1)S(1)} %get-tuple-element.773), channel_id=1, source_target_pairs={{8,0},{16,8},{24,16},{32,24},{40,32},{48,40},{56,48},{64,56},{72,6... | collective-permute-start | bytes 589832 | tf_op jit(solution)/shard_map/while/body/eval_jaxpr/ppermute | solution.py:15
  194.5 10.0 %collective-permute-start = (bf16[384,2,128]{2,0,1:T(8,128)(2,1)S(1)}, bf16[384,2,128]{2,0,1:T(8,128)(2,1)S(1)}, u32[]{:S(2)}, u32[]{:S(2)}) collective-permute-start(bf16[384,2,128]{2,0,1:T(8,128)(2,1)S(1)} %get-tuple-element.772), channel_id=1, source_target_pairs={{8,0},{16,8},{24,16},{32,24},{40,32},{48,40},{56,48},{64,56},{72,6... | collective-permute-start | bytes 589832 | tf_op jit(solution)/shard_map/while/body/eval_jaxpr/ppermute | solution.py:15
  197.0 9.1 %collective-permute-start.4 = (f32[384,2,128]{2,0,1:T(8,128)S(1)}, f32[384,2,128]{2,0,1:T(8,128)S(1)}, u32[]{:S(2)}, u32[]{:S(2)}) collective-permute-start(f32[384,2,128]{2,0,1:T(8,128)S(1)} %get-tuple-element.776), channel_id=1, source_target_pairs={{8,0},{16,8},{24,16},{32,24},{40,32},{48,40},{56,48},{64,56},{72,6... | collective-permute-start | bytes 1179656 | tf_op jit(solution)/shard_map/while/body/eval_jaxpr/ppermute | solution.py:21
  207.9 17.3 %collective-permute-start.5 = (bf16[384,2,128]{2,1,0:T(2,128)(2,1)S(1)}, bf16[384,2,128]{2,1,0:T(2,128)(2,1)S(1)}, u32[]{:S(2)}, u32[]{:S(2)}) collective-permute-start(bf16[384,2,128]{2,1,0:T(2,128)(2,1)S(1)} %copy.80), channel_id=1, source_target_pairs={{992,0},{1000,8},{1008,16},{1016,24},{0,32},{8,40},{16,48},{24,56}... | collective-permute-start | bytes 589832 | tf_op jit(solution)/shard_map/ppermute | solution.py:21
  (4 other events, 10.0 us)
Sparse Core Ops, SparseCore 0:
  10.7 97.2 all-gather.1
  207.7 96.5 all-reduce.4
where the time goes:
time: 316 us; the launch traced here: 314 us
  waiting for transfers between devices  185 us (59%)
  starting transfers between devices  64.9 us (21%)
  other arithmetic  19.9 us (6%)
  matrix products  15.3 us (5%)
  between operations  14.9 us (5%)
  local copies, waits for them, and re-layouts  14.2 us (4%)
    all_gather x1, waiting for transfers between devices, per_device(): lax.all_gather(grad_output, 'tp', axis=0, tiled=True)  94.9 us
    unnamed x3, waiting for transfers between devices  79 us
    ppermute x13, starting transfers between devices, from_behind(): return lax.ppermute(block, axis, route)  47 us
    ppermute x8, starting transfers between devices, passed_along(): return lax.ppermute(shard, axis, pairs)  17.7 us
    ppermute x13, waiting for transfers between devices, from_behind(): return lax.ppermute(block, axis, route)  10.5 us
    select_n x5, other arithmetic, doc_labels(): return jnp.repeat(labels, block_size, total_repeat_length=row_count)  9.77 us
    add x4, other arithmetic, pair_terms(): query_pos = query_rank * row_count + offsets  7.63 us
    unnamed x21, local copies, waits for them, and re-layouts  6.91 us
  transfers between devices with their start and end apart: 23, of which 3 were waited for; matrix products, arithmetic and copies ran while one was open for 11% of the time, Pallas kernels for 0%

commit v1 on v0

v1 whole, which is shorter than its diff:
```python
import functools

import jax
import jax.numpy as jnp
from jax import lax
from jax.experimental import pallas as pl
from jax.experimental.pallas import tpu as pltpu
from jax.sharding import PartitionSpec as P

F32 = jnp.float32
BF16 = jnp.bfloat16
MESH = pl.DeviceIdType.MESH
RANKS = 128
REACH = 4
ROWS = 384
PART = 48
HEAD = 128
WIDE = 256
D = 8192
HALF = D // 2
SUB = D // 8
NEG = -1e30
SCALE = HEAD ** -0.5
NT = (((1,), (1,)), ((), ()))


def ring_places():
    c = lax.axis_index("ctx")
    t = lax.axis_index("tp")
    return c, t


def gather_kernel(
    q_in, kv_in, lse_in, o_in, g_hbm, w_hbm,
    qw, kvw, lsew, dow, delw,
    wmine, woth, gbuf, xsend,
    loc_sem, g_ss, g_rs, w_ss, w_rs, s_ss, s_rs,
    q_ss, q_rs, l_ss, l_rs, kv_ss, kv_rs, x_ss, x_rs, do_ss, do_rs, de_ss, de_rs,
):
    c, t = ring_places()
    xlo = t // 4
    y = t % 4
    core = c % 2
    up = (c, xlo * 4 + (y + 1) % 4)
    down = (c, xlo * 4 + (y + 3) % 4)
    other = (t + 4) % 8
    lo = (c, other)
    hi = ((c + RANKS // 2) % RANKS, other)
    sib = (c + 1 - 2 * core, t)
    prev = ((c + RANKS - 1) % RANKS, t)
    nxt = ((c + 1) % RANKS, t)
    far = ((c + RANKS - 1 + 2 * core) % RANKS, t)

    barrier = pltpu.get_barrier_semaphore()
    for peer in (up, down, lo, hi, sib, far):
        pl.semaphore_signal(barrier, inc=1, device_id=peer, device_id_type=MESH)
    pl.semaphore_wait(barrier, 6)

    def remote(src, dst, ss, rs, peer):
        return pltpu.make_async_remote_copy(
            src_ref=src, dst_ref=dst, send_sem=ss, recv_sem=rs,
            device_id=peer, device_id_type=MESH,
        )

    A = pl.ds(0, HALF)
    B = pl.ds(HALF, HALF)

    def slot(s, cols):
        return gbuf.at[pl.ds(s * PART, PART), cols]

    g_up_a = remote(g_hbm.at[:, A], slot(1, A), g_ss.at[0], g_rs.at[0], up)
    g_up_b = remote(g_hbm.at[:, B], slot(1, B), g_ss.at[1], g_rs.at[1], up)
    g_up_f = remote(slot(1, A), slot(3, A), g_ss.at[2], g_rs.at[2], up)
    g_dn_b = remote(g_hbm.at[:, B], slot(2, B), g_ss.at[3], g_rs.at[3], down)
    g_dn_a = remote(g_hbm.at[:, A], slot(2, A), g_ss.at[4], g_rs.at[4], down)
    g_dn_f = remote(slot(2, B), slot(3, B), g_ss.at[5], g_rs.at[5], down)

    def wcols(link, k):
        return pl.ds(pl.multiple_of(core * 4096 + link * 2048 + k * SUB, SUB), SUB)

    w_sends, s_sends = [], []
    for k in range(2):
        for link, peer in ((0, lo), (1, hi)):
            i = 2 * k + link
            cols = wcols(link, k)
            w_sends.append(remote(w_hbm.at[:, cols], woth.at[:, cols], w_ss.at[i], w_rs.at[i], peer))
            s_sends.append(remote(woth.at[:, cols], woth.at[:, cols], s_ss.at[i], s_rs.at[i], sib))

    g_up_a.start()
    g_dn_b.start()
    w_sends[0].start()
    w_sends[1].start()
    g_up_b.start()
    g_dn_a.start()
    w_sends[2].start()
    w_sends[3].start()

    def back_ok(d):
        return jnp.logical_and(c >= 1, c + d <= RANKS - 1)

    def fwd_ok(d):
        return jnp.logical_and(c <= RANKS - 2, c - d >= 0)

    def q_copy(d):
        src = q_in if d == 0 else qw.at[d]
        return remote(src, qw.at[d + 1], q_ss.at[d], q_rs.at[d], prev)

    def l_copy(d):
        src = lse_in if d == 0 else lsew.at[d]
        return remote(src, lsew.at[d + 1], l_ss.at[d], l_rs.at[d], prev)

    def kv_copy(d):
        src = kv_in if d == 0 else kvw.at[d]
        return remote(src, kvw.at[d + 1], kv_ss.at[d], kv_rs.at[d], nxt)

    def do_copy(d, u):
        return remote(dow.at[d, u], dow.at[d + 1, u], do_ss.at[d, u], do_rs.at[d, u], prev)

    def de_copy(d):
        return remote(delw.at[d], delw.at[d + 1], de_ss.at[d], de_rs.at[d], prev)

    @pl.when(back_ok(0))
    def _():
        q_copy(0).start()
        l_copy(0).start()

    @pl.when(fwd_ok(0))
    def _():
        kv_copy(0).start()

    w_loc = pltpu.make_async_copy(w_hbm, wmine, loc_sem.at[0])
    g_loc = pltpu.make_async_copy(g_hbm, gbuf.at[pl.ds(0, PART), :], loc_sem.at[1])
    w_loc.start()
    g_loc.start()

    qw[0] = q_in[...]
    kvw[0] = kv_in[...]
    lsew[0] = lse_in[...]
    for d in range(1, REACH + 1):
        @pl.when(c + d > RANKS - 1)
        def _():
            qw[d] = jnp.zeros((ROWS, WIDE), BF16)
            lsew[d] = jnp.zeros((2, ROWS), F32)
            delw[d] = jnp.zeros((2, ROWS), F32)
            dow[d] = jnp.zeros((8, PART, WIDE), BF16)

        @pl.when(c - d < 0)
        def _():
            kvw[d] = jnp.zeros((ROWS, WIDE), BF16)

    def project(first, count, w):
        def body(k, acc):
            cols = pl.ds(pl.multiple_of(k * 1024, 1024), 1024)
            return acc + lax.dot_general(
                gbuf[first * PART:(first + count) * PART, cols], w[:, cols], NT,
                preferred_element_type=F32,
            )
        return lax.fori_loop(0, 8, body, jnp.zeros((count * PART, WIDE), F32)).astype(BF16)

    slot_y = (y, (y + 3) % 4, (y + 1) % 4, (y + 2) % 4)

    def mine(first, count):
        out = project(first, count, wmine)
        for s in range(first, first + count):
            dow[0, xlo * 4 + slot_y[s]] = out[(s - first) * PART:(s - first + 1) * PART]

    def x_copy(s):
        return remote(
            xsend.at[s], dow.at[0, xlo * 4 + slot_y[s]], x_ss.at[s], x_rs.at[s], lo)

    def theirs(first, count):
        out = project(first, count, woth)
        for s in range(first, first + count):
            xsend[s] = out[(s - first) * PART:(s - first + 1) * PART]
            x_copy(s).start()

    def chain_start(u):
        @pl.when(back_ok(0))
        def _():
            do_copy(0, u).start()

    def chain_forward(u):
        for d in range(1, REACH):
            @pl.when(c + d <= RANKS - 1)
            def _():
                do_copy(d - 1, u).wait_recv()

            @pl.when(back_ok(d))
            def _():
                do_copy(d, u).start()

    w_loc.wait()
    g_loc.wait()
    mine(0, 1)
    chain_start(xlo * 4 + slot_y[0])

    for d in range(1, REACH):
        @pl.when(c - d >= 0)
        def _():
            kv_copy(d - 1).wait_recv()

        @pl.when(fwd_ok(d))
        def _():
            kv_copy(d).start()

        @pl.when(c + d <= RANKS - 1)
        def _():
            q_copy(d - 1).wait_recv()
            l_copy(d - 1).wait_recv()

        @pl.when(back_ok(d))
        def _():
            q_copy(d).start()
            l_copy(d).start()

    g_up_a.wait_recv()
    g_up_f.start()
    g_dn_b.wait_recv()
    g_dn_f.start()
    for i in range(2):
        w_sends[i].wait_recv()
        s_sends[i].start()
    chain_forward(xlo * 4 + slot_y[0])
    g_up_b.wait_recv()
    g_dn_a.wait_recv()
    mine(1, 2)
    chain_start(xlo * 4 + slot_y[1])
    chain_start(xlo * 4 + slot_y[2])
    chain_forward(xlo * 4 + slot_y[1])
    chain_forward(xlo * 4 + slot_y[2])
    for i in range(2, 4):
        w_sends[i].wait_recv()
        s_sends[i].start()
    for i in range(4):
        s_sends[i].wait_recv()
    theirs(0, 3)
    g_up_f.wait_recv()
    g_dn_f.wait_recv()
    theirs(3, 1)
    mine(3, 1)
    chain_start(xlo * 4 + slot_y[3])
    for s in range(4):
        x_copy(s).wait_recv()
        chain_start((1 - xlo) * 4 + slot_y[s])

    ones = jnp.ones((8, HEAD), F32)
    for h in range(2):
        lanes = slice(h * HEAD, (h + 1) * HEAD)
        own = dow[0].reshape(ROWS, WIDE)[:, lanes].astype(F32)
        prod = own * o_in[:, lanes].astype(F32)
        row = lax.dot_general(ones, prod, NT, precision=lax.Precision.HIGHEST,
                              preferred_element_type=F32)
        delw[0, h:h + 1, :] = row[0:1]

    @pl.when(back_ok(0))
    def _():
        de_copy(0).start()

    chain_forward(xlo * 4 + slot_y[3])
    for s in range(4):
        chain_forward((1 - xlo) * 4 + slot_y[s])
    for d in range(1, REACH):
        @pl.when(c + d <= RANKS - 1)
        def _():
            de_copy(d - 1).wait_recv()

        @pl.when(back_ok(d))
        def _():
            de_copy(d).start()

    last = REACH - 1

    @pl.when(c + REACH <= RANKS - 1)
    def _():
        q_copy(last).wait_recv()
        l_copy(last).wait_recv()
        de_copy(last).wait_recv()
        for u in range(8):
            do_copy(last, u).wait_recv()

    @pl.when(c - REACH >= 0)
    def _():
        kv_copy(last).wait_recv()

    for cp in (g_up_a, g_up_b, g_up_f, g_dn_a, g_dn_b, g_dn_f, *w_sends, *s_sends):
        cp.wait_send()
    for s in range(4):
        x_copy(s).wait_send()
    for d in range(REACH):
        @pl.when(back_ok(d))
        def _():
            q_copy(d).wait_send()
            l_copy(d).wait_send()
            de_copy(d).wait_send()
            for u in range(8):
                do_copy(d, u).wait_send()

        @pl.when(fwd_ok(d))
        def _():
            kv_copy(d).wait_send()


def attend_kernel(
    qw, kvw, lsew, dow, delw, docs,
    dq_out, dkv_out,
    part, land, ss, rs,
):
    c, t = ring_places()
    xlo = t // 4
    barrier = pltpu.get_barrier_semaphore()
    for step in range(1, 8):
        pl.semaphore_signal(barrier, inc=1, device_id=(c, (t + step) % 8), device_id_type=MESH)
    pl.semaphore_wait(barrier, 7)

    lane_blk = lax.broadcasted_iota(jnp.int32, (1, ROWS), 1) // HEAD

    def doc_at(block):
        return docs[jnp.clip(block, 0, 3 * RANKS - 1)]

    def bias_row(mine, far_rank, first):
        vals = []
        for b in range(3):
            same = doc_at(far_rank * 3 + b) == mine
            ok = jnp.logical_and(same, jnp.logical_and(far_rank >= 0, far_rank < RANKS))
            vals.append(jnp.where(ok, 0.0, NEG).astype(F32))
        return jnp.where(lane_blk == 0, vals[0], jnp.where(lane_blk == 1, vals[1], vals[2]))

    for kb in range(3):
        k_doc = docs[c * 3 + kb]
        k = kvw[0, kb * HEAD:(kb + 1) * HEAD, 0:HEAD]
        v = kvw[0, kb * HEAD:(kb + 1) * HEAD, HEAD:WIDE]
        k_pos = lax.broadcasted_iota(jnp.int32, (HEAD, ROWS), 0) + kb * HEAD
        q_pos = lax.broadcasted_iota(jnp.int32, (HEAD, ROWS), 1)

        def step(d, carry, k=k, v=v, k_doc=k_doc, k_pos=k_pos, q_pos=q_pos):
            dk, dv = carry
            row = bias_row(k_doc, c + d, 0)
            causal = (k_pos <= q_pos + d * ROWS)
            for h in range(2):
                lanes = slice(h * HEAD, (h + 1) * HEAD)
                q = qw[d, :, lanes]
                do = dow[d, :, lanes]
                s = lax.dot_general(k, q, NT, preferred_element_type=F32)
                x = s * SCALE + (row - lsew[d, h:h + 1, :])
                p = jnp.exp(jnp.where(causal, x, NEG))
                dp = lax.dot_general(v, do, NT, preferred_element_type=F32)
                ds = (p * (dp - delw[d, h:h + 1, :]) * SCALE).astype(BF16)
                dk = dk + jnp.dot(ds, q, preferred_element_type=F32)
                dv = dv + jnp.dot(p.astype(BF16), do, preferred_element_type=F32)
            return dk, dv

        zero = jnp.zeros((HEAD, HEAD), F32)
        dk, dv = lax.fori_loop(0, REACH + 1, step, (zero, zero))
        part[kb * HEAD:(kb + 1) * HEAD, 0:HEAD] = dk.astype(BF16)
        part[kb * HEAD:(kb + 1) * HEAD, HEAD:WIDE] = dv.astype(BF16)

    def send(step):
        to = (t + step) % 8
        return pltpu.make_async_remote_copy(
            src_ref=part.at[pl.ds(pl.multiple_of(to * PART, PART), PART)],
            dst_ref=land.at[step],
            send_sem=ss.at[step], recv_sem=rs.at[step],
            device_id=(c, to), device_id_type=MESH)

    for step in range(1, 8):
        send(step).start()

    for h in range(2):
        lse_col = jnp.broadcast_to(lsew[0, h:h + 1, :], (HEAD, ROWS)).T
        del_col = jnp.broadcast_to(delw[0, h:h + 1, :], (HEAD, ROWS)).T
        lanes = slice(h * HEAD, (h + 1) * HEAD)
        for qb in range(3):
            q_doc = docs[c * 3 + qb]
            rows = slice(qb * HEAD, (qb + 1) * HEAD)
            q = qw[0, rows, lanes]
            do = dow[0, rows, lanes]
            lse = jnp.concatenate([lse_col[rows]] * 3, axis=1)
            dl = jnp.concatenate([del_col[rows]] * 3, axis=1)
            q_pos = lax.broadcasted_iota(jnp.int32, (HEAD, ROWS), 0) + qb * HEAD
            k_pos = lax.broadcasted_iota(jnp.int32, (HEAD, ROWS), 1)

            def step(d, dq, q=q, do=do, lse=lse, dl=dl, q_doc=q_doc, q_pos=q_pos, k_pos=k_pos):
                row = bias_row(q_doc, c - d, 0)
                k = kvw[d, :, 0:HEAD]
                v = kvw[d, :, HEAD:WIDE]
                s = lax.dot_general(q, k, NT, preferred_element_type=F32)
                x = s * SCALE + (row - lse)
                p = jnp.exp(jnp.where(k_pos <= q_pos + d * ROWS, x, NEG))
                dp = lax.dot_general(do, v, NT, preferred_element_type=F32)
                ds = (p * (dp - dl) * SCALE).astype(BF16)
                return dq + jnp.dot(ds, k, preferred_element_type=F32)

            dq = lax.fori_loop(0, REACH + 1, step, jnp.zeros((HEAD, HEAD), F32))
            dq_out[h, rows, :] = dq.astype(BF16)

    totals = [jnp.zeros((PART, WIDE), F32), jnp.zeros((PART, WIDE), F32)]
    own = part[pl.ds(pl.multiple_of(t * PART, PART), PART), :].astype(F32)
    for step in range(8):
        if step == 0:
            got = own
        else:
            send(step).wait_recv()
            got = land[step].astype(F32)
        src_lo = ((t + 8 - step) % 8) // 4
        w1 = src_lo.astype(F32)
        totals[0] = totals[0] + got * (1.0 - w1)
        totals[1] = totals[1] + got * w1
    for g in range(2):
        dkv_out[g] = totals[g].astype(BF16)
    for step in range(1, 8):
        send(step).wait_send()


def per_device(queries, key_tensor, value_tensor, attn_output, lse, grad_output, out_proj, block_doc):
    group = lax.axis_index("tp") // 4
    q2 = queries.reshape(ROWS, WIDE)
    o2 = attn_output.reshape(ROWS, WIDE)
    kv = jnp.concatenate(
        [
            lax.dynamic_index_in_dim(key_tensor, group, 1, keepdims=False),
            lax.dynamic_index_in_dim(value_tensor, group, 1, keepdims=False),
        ],
        axis=1,
    )
    vmem = pl.BlockSpec(memory_space=pltpu.VMEM)
    hbm = pl.BlockSpec(memory_space=pl.ANY)
    dma = pltpu.SemaphoreType.DMA
    span = REACH + 1
    qw, kvw, lsew, dow, delw = pl.pallas_call(
        gather_kernel,
        out_shape=(
            jax.ShapeDtypeStruct((span, ROWS, WIDE), BF16),
            jax.ShapeDtypeStruct((span, ROWS, WIDE), BF16),
            jax.ShapeDtypeStruct((span, 2, ROWS), F32),
            jax.ShapeDtypeStruct((span, 8, PART, WIDE), BF16),
            jax.ShapeDtypeStruct((span, 2, ROWS), F32),
        ),
        in_specs=[vmem, vmem, vmem, vmem, hbm, hbm],
        out_specs=(vmem,) * 5,
        scratch_shapes=[
            pltpu.VMEM((WIDE, D), BF16),
            pltpu.VMEM((WIDE, D), BF16),
            pltpu.VMEM((4 * PART, D), BF16),
            pltpu.VMEM((4, PART, WIDE), BF16),
            dma((2,)), dma((6,)), dma((6,)), dma((4,)), dma((4,)), dma((4,)), dma((4,)),
            dma((4,)), dma((4,)), dma((4,)), dma((4,)), dma((4,)), dma((4,)),
            dma((4,)), dma((4,)), dma((4, 8)), dma((4, 8)), dma((4,)), dma((4,)),
        ],
        compiler_params=pltpu.CompilerParams(
            collective_id=0, has_side_effects=True, vmem_limit_bytes=40 << 20),
        name="gather_project",
    )(q2, kv, lse, o2, grad_output, out_proj)
    dq, dkv = pl.pallas_call(
        attend_kernel,
        out_shape=(
            jax.ShapeDtypeStruct((2, ROWS, HEAD), BF16),
            jax.ShapeDtypeStruct((2, PART, WIDE), BF16),
        ),
        in_specs=[vmem] * 5 + [pl.BlockSpec(memory_space=pltpu.SMEM)],
        out_specs=(vmem, vmem),
        scratch_shapes=[
            pltpu.VMEM((ROWS, WIDE), BF16),
            pltpu.VMEM((8, PART, WIDE), BF16),
            dma((8,)), dma((8,)),
        ],
        compiler_params=pltpu.CompilerParams(
            collective_id=1, has_side_effects=True, vmem_limit_bytes=40 << 20),
        name="attend_reduce",
    )(qw, kvw, lsew, dow.reshape(span, ROWS, WIDE), delw, block_doc)
    grad_query = jnp.transpose(dq, (1, 0, 2))
    grad_key = jnp.transpose(dkv[:, :, :HEAD], (1, 0, 2))
    grad_value = jnp.transpose(dkv[:, :, HEAD:], (1, 0, 2))
    return grad_query, grad_key, grad_value


def solution(mesh):
    placed = (
        P("ctx", "tp", None),
        P("ctx", None, None),
        P("ctx", None, None),
        P("ctx", "tp", None),
        P("tp", "ctx"),
        P(("ctx", "tp"), None),
        P("tp", None),
        P(),
    )
    return jax.shard_map(
        per_device,
        mesh=mesh,
        in_specs=placed,
        out_specs=(
            P("ctx", "tp", None),
            P(("ctx", "tp"), None, None),
            P(("ctx", "tp"), None, None),
        ),
        check_vma=False,
    )
```

time: 316 us -> 119 us (0.38)
  the two profiles are of different devices: /device:TPU:4 before, /device:TPU:97 now
where the time goes in v1:
time: 119 us; the launch traced here: 118 us
  Pallas kernels  109 us (92%)
  local copies, waits for them, and re-layouts  8.69 us (7%)
    pallas_call x1, Pallas kernels, per_device(): pl.pallas_call(gather_kernel, out_shape=(jax.ShapeDtypeStruct((span, ROWS...  84.9 us
    pallas_call x1, Pallas kernels, per_device(): pl.pallas_call(attend_kernel, out_shape=(jax.ShapeDtypeStruct((2, ROWS, H...  24.1 us
    unnamed x13, local copies, waits for them, and re-layouts  6.17 us

profile of v1, /device:TPU:97, one launch (start us, length us, event | category | flops | bytes accessed | tf_op | source)
XLA Modules:
  0.0 118.4 jit_solution(4294512523348448386)
XLA Ops:
  0.6 0.0 copy-start.3
  0.7 1.4 %constant_dynamic-slice_fusion = (bf16[384,1,128]{2,1,0:T(2,128)(2,1)S(1)}, bf16[384,1,128]{2,1,0:T(2,128)(2,1)S(1)}) fusion(bf16[384,2,128]{2,1,0:T(2,128)(2,1)} %param.10, s32[]{:T(128)S(6)} %select_n.11, bf16[384,2,128]{2,1,0:T(2,128)(2,1)} %param.9), kind=kLoop, calls=%fused_computation.7 | loop fusion | bytes 393220 | tf_op jit(solution)/shard_map/jit(dynamic_index_in_dim)/dynamic_slice | solution.py:421
  2.2 1.1 copy_bitcast_fusion
  3.3 0.0 copy-start
  3.3 2.2 %copy-done = bf16[256,8192]{1,0:T(8,128)(2,1)S(1)} copy-done((bf16[256,8192]{1,0:T(8,128)(2,1)S(1)}, bf16[256,8192]{1,0:T(8,128)(2,1)}, u32[]{:S(2)}) %copy-start) | copy-done | bytes 4194328
  5.4 0.0 copy-start.1
  5.5 1.1 copy-done.1
  6.6 0.0 copy-start.2
  6.6 0.7 copy-done.2
  7.3 84.9 %gather_project.1 = (bf16[5,384,256]{2,1,0:T(8,128)(2,1)S(1)}, bf16[5,384,256]{2,1,0:T(8,128)(2,1)S(1)}, f32[5,2,384]{2,1,0:T(2,128)S(1)}, bf16[5,8,48,256]{3,2,1,0:T(8,128)(2,1)S(1)}, f32[5,2,384]{2,1,0:T(2,128)S(1)}) custom-call(bf16[384,256]{1,0:T(8,128)(2,1)S(1)} %get-tuple-element.28.q_in, bf16[384,256]{1,0:T(8,128)(2,1)S(1)} %pad_maximum_fusion.kv_in, ...), custom_call_target="tpu_custom_call" | custom-call | tf_op jit(solution)/shard_map/gather_project/pallas_call | solution.py:429
  92.2 0.0 copy-done.3
  92.2 24.1 %attend_reduce.1 = (bf16[2,384,128]{2,1,0:T(8,128)(2,1)S(1)}, bf16[2,48,256]{2,1,0:T(8,128)(2,1)S(1)}) custom-call(bf16[5,384,256]{2,1,0:T(8,128)(2,1)S(1)} %get-tuple-element.10.qw, bf16[5,384,256]{2,1,0:T(8,128)(2,1)S(1)} %get-tuple-element.11.kvw, f32[5,2,384]{2,1,0:T(2,128)S(1)} %get-tuple-element.12.lsew, bf16[5,384,256]{2,1,0:T(8,128)(2,1)S(1)} %bitcast.18, ...), custom_call_target="tpu_custom_call" | custom-call | tf_op jit(solution)/shard_map/attend_reduce/pallas_call | solution.py:453
  116.2 0.9 copy.16
  117.1 0.6 copy.18
  117.8 0.6 copy.17
  (4 shorter events, 0.1 us)
Async XLA Ops:
  0.6 91.5 %copy-start.3 = (s32[384]{0:T(512)S(1)}, s32[384]{0:T(512)}, u32[]{:S(2)}) copy-start(s32[384]{0:T(512)} %docs.1) | copy-start | bytes 4612
  3.3 2.2 %copy-start = (bf16[256,8192]{1,0:T(8,128)(2,1)S(1)}, bf16[256,8192]{1,0:T(8,128)(2,1)}, u32[]{:S(2)}) copy-start(bf16[256,8192]{1,0:T(8,128)(2,1)} %w_hbm.1) | copy-start | bytes 12582916
  5.4 1.1 copy-start.1
  6.6 0.7 copy-start.2

commit v2 on v1

v2 whole, which is shorter than its diff:
```python
import jax
import jax.numpy as jnp
from jax import lax
from jax.experimental import pallas as pl
from jax.experimental.pallas import tpu as pltpu
from jax.sharding import PartitionSpec as P

F32 = jnp.float32
BF16 = jnp.bfloat16
MESH = pl.DeviceIdType.MESH
RANKS = 128
REACH = 4
ROWS = 384
PART = 48
HEAD = 128
WIDE = 256
D = 8192
HALF = D // 2
QUARTER = D // 4
SUB = D // 8
NEG = -1e30
SCALE = HEAD ** -0.5
NT = (((1,), (1,)), ((), ()))


def ring_places():
    c = lax.axis_index("ctx")
    t = lax.axis_index("tp")
    return c, t


def fused_kernel(
    docs, q_in, kv_in, lse_in, o_hbm, g_hbm, w_hbm,
    dq_out, dkv_out,
    qw, kvw, lsew, dow, delw, o_in, lsec, delc,
    wmine, woth, gbuf, xsend, acc_t, acc_m, dk_acc, dv_acc, dq_acc, part, land,
    loc_sem, g_ss, g_rs, w_ss, w_rs, s_ss, s_rs,
    q_ss, q_rs, l_ss, l_rs, kv_ss, kv_rs, x_ss, x_rs, do_ss, do_rs, de_ss, de_rs,
    r_ss, r_rs, ready,
    rq, rl, rkv, rdo, rde, rq_rs, rl_rs, rkv_rs, rdo_rs, rde_rs,
):
    c, t = ring_places()
    xlo = t // 4
    y = t % 4
    core = c % 2
    up = (c, xlo * 4 + (y + 1) % 4)
    down = (c, xlo * 4 + (y + 3) % 4)
    other = (t + 4) % 8
    lo = (c, other)
    hi = ((c + RANKS // 2) % RANKS, other)
    sib = (c + 1 - 2 * core, t)
    prev = ((c + RANKS - 1) % RANKS, t)
    nxt = ((c + 1) % RANKS, t)
    far = ((c + RANKS - 1 + 2 * core) % RANKS, t)
    first = c == 0
    final = c == RANKS - 1
    before_seam = c == RANKS // 2 - 1
    after_seam = c == RANKS // 2
    inner = jnp.logical_not(first | final | before_seam | after_seam)

    barrier = pltpu.get_barrier_semaphore()

    def greet(peer):
        pl.semaphore_signal(barrier, inc=1, device_id=peer, device_id_type=MESH)

    for step in range(1, 8):
        greet((c, (t + step) % 8))
    greet(hi)
    greet(sib)

    @pl.when(inner)
    def _():
        greet(far)

    @pl.when(first)
    def _():
        greet((RANKS // 2 - 1, other))

    @pl.when(after_seam)
    def _():
        greet((RANKS - 1, other))

    lone = jnp.logical_or(first, after_seam)

    @pl.when(lone)
    def _():
        pl.semaphore_wait(barrier, 9)

    @pl.when(jnp.logical_not(lone))
    def _():
        pl.semaphore_wait(barrier, 10)

    @pl.when(before_seam)
    def _():
        pl.semaphore_signal(ready, inc=1, device_id=(0, other), device_id_type=MESH)

    def remote(src, dst, ss, rs, peer):
        return pltpu.make_async_remote_copy(
            src_ref=src, dst_ref=dst, send_sem=ss, recv_sem=rs,
            device_id=peer, device_id_type=MESH,
        )

    A = pl.ds(0, HALF)
    B = pl.ds(HALF, HALF)

    def slot(s, cols):
        return gbuf.at[pl.ds(s * PART, PART), cols]

    g_up_a = remote(g_hbm.at[:, A], slot(1, A), g_ss.at[0], g_rs.at[0], up)
    g_up_b = remote(g_hbm.at[:, B], slot(1, B), g_ss.at[1], g_rs.at[1], up)
    g_dn_b = remote(g_hbm.at[:, B], slot(2, B), g_ss.at[2], g_rs.at[2], down)
    g_dn_a = remote(g_hbm.at[:, A], slot(2, A), g_ss.at[3], g_rs.at[3], down)
    g_up_f, g_dn_f = [], []
    for i in range(2):
        ca = pl.ds(i * QUARTER, QUARTER)
        cb = pl.ds(HALF + i * QUARTER, QUARTER)
        g_up_f.append(remote(slot(1, ca), slot(3, ca), g_ss.at[4 + i], g_rs.at[4 + i], up))
        g_dn_f.append(remote(slot(2, cb), slot(3, cb), g_ss.at[6 + i], g_rs.at[6 + i], down))

    def wcols(link, k):
        return pl.ds(pl.multiple_of(core * 4096 + link * 2048 + k * SUB, SUB), SUB)

    w_sends, s_sends = [], []
    for k in range(2):
        for link, peer in ((0, lo), (1, hi)):
            i = 2 * k + link
            cols = wcols(link, k)
            w_sends.append(remote(w_hbm.at[:, cols], woth.at[:, cols], w_ss.at[i], w_rs.at[i], peer))
            s_sends.append(remote(woth.at[:, cols], woth.at[:, cols], s_ss.at[i], s_rs.at[i], sib))

    g_up_a.start()
    g_dn_b.start()
    w_sends[0].start()
    w_sends[1].start()
    g_up_b.start()
    g_dn_a.start()
    w_sends[2].start()
    w_sends[3].start()

    def back_ok(d):
        return jnp.logical_and(c >= 1, c + d <= RANKS - 1)

    def fwd_ok(d):
        return jnp.logical_and(c <= RANKS - 2, c - d >= 0)

    def q_copy(d):
        src = q_in if d == 0 else qw.at[d]
        return remote(src, qw.at[d + 1], q_ss.at[d], q_rs.at[d], prev)

    def l_copy(d):
        src = lse_in if d == 0 else lsew.at[d]
        return remote(src, lsew.at[d + 1], l_ss.at[d], l_rs.at[d], prev)

    def kv_copy(d):
        src = kv_in if d == 0 else kvw.at[d]
        return remote(src, kvw.at[d + 1], kv_ss.at[d], kv_rs.at[d], nxt)

    def do_copy(d, u):
        return remote(dow.at[d, u], dow.at[d + 1, u], do_ss.at[d, u], do_rs.at[d, u], prev)

    def de_copy(d):
        return remote(delw.at[d], delw.at[d + 1], de_ss.at[d], de_rs.at[d], prev)

    def q_src(d):
        return q_in if isinstance(d, int) and d == 0 else qw.at[d]

    def l_src(d):
        return lse_in if isinstance(d, int) and d == 0 else lsew.at[d]

    def kv_src(d):
        return kv_in if isinstance(d, int) and d == 0 else kvw.at[d]

    def send_q(d, when):
        ok = jnp.logical_and(when, back_ok(d))

        @pl.when(jnp.logical_and(ok, jnp.logical_not(after_seam)))
        def _():
            q_copy(d).start()
            l_copy(d).start()

        @pl.when(jnp.logical_and(ok, after_seam))
        def _():
            remote(q_src(d), rq.at[d], q_ss.at[d], rq_rs.at[d], hi).start()
            remote(l_src(d), rl.at[d], l_ss.at[d], rl_rs.at[d], hi).start()

    def send_kv(d, when):
        ok = jnp.logical_and(when, fwd_ok(d))

        @pl.when(jnp.logical_and(ok, jnp.logical_not(before_seam)))
        def _():
            kv_copy(d).start()

        @pl.when(jnp.logical_and(ok, before_seam))
        def _():
            remote(kv_src(d), rkv.at[d], kv_ss.at[d], rkv_rs.at[d], hi).start()

    def send_units(units, d, when):
        ok = jnp.logical_and(when, back_ok(d))

        @pl.when(jnp.logical_and(ok, jnp.logical_not(after_seam)))
        def _():
            for u in units:
                do_copy(d, u).start()

        @pl.when(jnp.logical_and(ok, after_seam))
        def _():
            for u in units:
                remote(dow.at[d, u], rdo.at[d, u], do_ss.at[d, u], rdo_rs.at[d, u], hi).start()

    def send_delta(d, when):
        ok = jnp.logical_and(when, back_ok(d))

        @pl.when(jnp.logical_and(ok, jnp.logical_not(after_seam)))
        def _():
            de_copy(d).start()

        @pl.when(jnp.logical_and(ok, after_seam))
        def _():
            remote(delw.at[d], rde.at[d], de_ss.at[d], rde_rs.at[d], hi).start()

    back_to = (RANKS // 2 - 1, other)
    on_to = (RANKS // 2, other)

    def relay_q(d):
        return (remote(rq.at[d], qw.at[d + 1], q_ss.at[d], q_rs.at[d], back_to),
                remote(rl.at[d], lsew.at[d + 1], l_ss.at[d], l_rs.at[d], back_to))

    def relay_q_in(d):
        return (remote(rq.at[d], rq.at[d], q_ss.at[d], rq_rs.at[d], hi),
                remote(rl.at[d], rl.at[d], l_ss.at[d], rl_rs.at[d], hi))

    def relay_units(units, d):
        for u in units:
            remote(rdo.at[d, u], rdo.at[d, u], do_ss.at[d, u], rdo_rs.at[d, u], hi).wait_recv()
            remote(rdo.at[d, u], dow.at[d + 1, u], do_ss.at[d, u], do_rs.at[d, u], back_to).start()

    def relay_delta(d):
        remote(rde.at[d], rde.at[d], de_ss.at[d], rde_rs.at[d], hi).wait_recv()
        remote(rde.at[d], delw.at[d + 1], de_ss.at[d], de_rs.at[d], back_to).start()

    def relay_kv(d):
        remote(rkv.at[d], rkv.at[d], kv_ss.at[d], rkv_rs.at[d], hi).wait_recv()
        remote(rkv.at[d], kvw.at[d + 1], kv_ss.at[d], kv_rs.at[d], on_to).start()

    send_q(0, True)
    send_kv(0, True)

    w_loc = pltpu.make_async_copy(w_hbm, wmine, loc_sem.at[0])
    g_loc = pltpu.make_async_copy(g_hbm, gbuf.at[pl.ds(0, PART), :], loc_sem.at[1])
    locals_ = [
        pltpu.make_async_copy(q_in, qw.at[0], loc_sem.at[2]),
        pltpu.make_async_copy(kv_in, kvw.at[0], loc_sem.at[3]),
        pltpu.make_async_copy(lse_in, lsew.at[0], loc_sem.at[4]),
        pltpu.make_async_copy(o_hbm, o_in, loc_sem.at[5]),
    ]
    w_loc.start()
    g_loc.start()
    for cp in locals_:
        cp.start()
    for d in range(1, REACH + 1):
        @pl.when(c + d > RANKS - 1)
        def _():
            qw[d] = jnp.zeros((ROWS, WIDE), BF16)
            lsew[d] = jnp.zeros((2, ROWS), F32)
            delw[d] = jnp.zeros((2, ROWS), F32)
            dow[d] = jnp.zeros((8, PART, WIDE), BF16)

        @pl.when(c - d < 0)
        def _():
            kvw[d] = jnp.zeros((ROWS, WIDE), BF16)

    def partial_product(first, count, w, starts, width):
        total = None
        for start in starts:
            cols = slice(start, start + width)
            one = lax.dot_general(
                gbuf[first * PART:(first + count) * PART, cols], w[:, cols], NT,
                preferred_element_type=F32)
            total = one if total is None else total + one
        return total

    even = (0, 2048, 4096, 6144)
    odd = (1024, 3072, 5120, 7168)
    slot_y = (y, (y + 3) % 4, (y + 1) % 4, (y + 2) % 4)
    own_unit = [xlo * 4 + v for v in slot_y]
    mate_unit = [(1 - xlo) * 4 + v for v in slot_y]
    early_units = own_unit[:3]
    middle_units = mate_unit[:3]
    late_units = [own_unit[3], mate_unit[3]]

    def mine(first, count):
        out = partial_product(first, count, wmine, (0,), D).astype(BF16)
        for s in range(first, first + count):
            dow[0, own_unit[s]] = out[(s - first) * PART:(s - first + 1) * PART]

    def x_copy(s):
        return remote(xsend.at[s], dow.at[0, own_unit[s]], x_ss.at[s], x_rs.at[s], lo)

    def forward_units(units, d):
        @pl.when(c + d <= RANKS - 1)
        def _():
            for u in units:
                do_copy(d - 1, u).wait_recv()

        send_units(units, d, True)

    def forward_kv(d, when):
        @pl.when(jnp.logical_and(when, c - d >= 0))
        def _():
            kv_copy(d - 1).wait_recv()

        send_kv(d, when)

    w_loc.wait()
    g_loc.wait()
    for cp in locals_:
        cp.wait()
    mine(0, 1)
    send_units(early_units[:1], 0, True)

    seam = RANKS // 2

    def q_over(d):
        return jnp.logical_and(c < seam, c + d >= seam)


    def kv_over(d):
        return jnp.logical_and(c >= seam, c - d < seam)


    def forward_q(d, when):
        @pl.when(jnp.logical_and(when, c + d <= RANKS - 1))
        def _():
            q_copy(d - 1).wait_recv()
            l_copy(d - 1).wait_recv()

        send_q(d, when)

    for d in range(1, REACH):
        forward_q(d, jnp.logical_not(q_over(d)))
        forward_kv(d, jnp.logical_not(kv_over(d)))

    g_up_a.wait_recv()
    g_dn_b.wait_recv()
    for i in range(2):
        g_up_f[i].start()
        g_dn_f[i].start()
    @pl.when(final)
    def _():
        for d in range(REACH):
            relay_kv(d)

    for h in range(2):
        lsec[h] = jnp.broadcast_to(lsew[0, h:h + 1, :], (HEAD, ROWS)).T
    for i in range(2):
        w_sends[i].wait_recv()
        s_sends[i].start()

    g_up_b.wait_recv()
    g_dn_a.wait_recv()
    mine(1, 2)

    send_units(early_units[1:], 0, True)
    for i in range(2):
        s_sends[i].wait_recv()
    acc_t[0:3 * PART, :] = partial_product(0, 3, woth, even, SUB)

    @pl.when(first)
    def _():
        pl.semaphore_wait(ready, 1)
        for d in range(REACH):
            for one, two in zip(relay_q_in(d), relay_q(d)):
                one.wait_recv()
                two.start()
        relay_units(mate_unit[:3], 0)

    forward_units(early_units, 1)
    forward_q(1, q_over(1))
    g_up_f[0].wait_recv()
    g_dn_f[0].wait_recv()
    acc_m[...] = partial_product(3, 1, wmine, (0, HALF), QUARTER)
    for i in range(2, 4):
        w_sends[i].wait_recv()
        s_sends[i].start()
    forward_units(early_units, 2)
    forward_q(2, q_over(2))
    for i in range(2, 4):
        s_sends[i].wait_recv()
    out = (acc_t[0:3 * PART, :] + partial_product(0, 3, woth, odd, SUB)).astype(BF16)
    for s in range(3):
        xsend[s] = out[s * PART:(s + 1) * PART]
        x_copy(s).start()
    acc_t[3 * PART:, :] = partial_product(3, 1, woth, (0, HALF), QUARTER)
    g_up_f[1].wait_recv()
    g_dn_f[1].wait_recv()
    later = (QUARTER, HALF + QUARTER)
    xsend[3] = (acc_t[3 * PART:, :] + partial_product(3, 1, woth, later, QUARTER)).astype(BF16)
    x_copy(3).start()
    for u in range(3):
        x_copy(u).wait_recv()
    send_units(middle_units, 0, True)
    dow[0, own_unit[3]] = (acc_m[...] + partial_product(3, 1, wmine, later, QUARTER)).astype(BF16)
    send_units(own_unit[3:], 0, True)
    forward_units(middle_units, 1)
    x_copy(3).wait_recv()
    send_units(mate_unit[3:], 0, True)

    ones = jnp.ones((8, HEAD), F32)
    for h in range(2):
        lanes = slice(h * HEAD, (h + 1) * HEAD)
        own = dow[0, :, :, lanes].reshape(ROWS, HEAD).astype(F32)
        prod = own * o_in[:, lanes].astype(F32)
        row = lax.dot_general(ones, prod, NT, precision=lax.Precision.HIGHEST,
                              preferred_element_type=F32)
        delw[0, h:h + 1, :] = row[0:1]
        delc[h] = jnp.broadcast_to(jnp.sum(prod, axis=1, keepdims=True), (ROWS, HEAD))

    send_delta(0, True)

    forward_units(early_units, 3)
    forward_q(3, q_over(3))
    for d in range(1, REACH):
        forward_kv(d, kv_over(d))

    lane_blk = lax.broadcasted_iota(jnp.int32, (1, ROWS), 1) // HEAD

    def bias_row(mine_doc, far_rank):
        vals = []
        for b in range(3):
            block = jnp.clip(far_rank * 3 + b, 0, 3 * RANKS - 1)
            inside = jnp.logical_and(far_rank >= 0, far_rank < RANKS)
            ok = jnp.logical_and(docs[block] == mine_doc, inside)
            vals.append(jnp.where(ok, 0.0, NEG).astype(F32))
        return jnp.where(lane_blk == 0, vals[0], jnp.where(lane_blk == 1, vals[1], vals[2]))

    def blocks(x):
        return [x[b * HEAD:(b + 1) * HEAD] for b in range(3)]

    def below():
        return (lax.broadcasted_iota(jnp.int32, (ROWS, ROWS), 0)
                <= lax.broadcasted_iota(jnp.int32, (ROWS, ROWS), 1))

    def key_side(d):
        k = kvw[0, :, 0:HEAD]
        v = kvw[0, :, HEAD:WIDE]
        rows = [bias_row(docs[c * 3 + b], c + d) for b in range(3)]
        for h in range(2):
            lanes = slice(h * HEAD, (h + 1) * HEAD)
            q = qw[d, :, lanes]
            do = dow[d, :, :, lanes].reshape(ROWS, HEAD)
            lse = lsew[d, h:h + 1, :]
            s = lax.dot_general(k, q, NT, preferred_element_type=F32)
            x = jnp.concatenate(
                [sb * SCALE + (row - lse) for sb, row in zip(blocks(s), rows)], axis=0)
            if isinstance(d, int) and d == 0:
                x = jnp.where(below(), x, NEG)
            p = jnp.exp(x)
            dp = lax.dot_general(v, do, NT, preferred_element_type=F32)
            ds = (p * (dp - delw[d, h:h + 1, :]) * SCALE).astype(BF16)
            dk = jnp.dot(ds, q, preferred_element_type=F32)
            dv = jnp.dot(p.astype(BF16), do, preferred_element_type=F32)
            if isinstance(d, int) and h == 0:
                dk_acc[...] = dk
                dv_acc[...] = dv
            else:
                dk_acc[...] += dk
                dv_acc[...] += dv

    def query_side(d):
        k = kvw[d, :, 0:HEAD]
        v = kvw[d, :, HEAD:WIDE]
        rows = [bias_row(docs[c * 3 + b], c - d) for b in range(3)]
        for h in range(2):
            lanes = slice(h * HEAD, (h + 1) * HEAD)
            q = qw[0, :, lanes]
            do = dow[0, :, :, lanes].reshape(ROWS, HEAD)
            lse = lsec[h]
            dl = delc[h]
            s = lax.dot_general(q, k, NT, preferred_element_type=F32)
            lse3 = jnp.concatenate([lse] * 3, axis=1)
            dl3 = jnp.concatenate([dl] * 3, axis=1)
            x = jnp.concatenate(
                [sb * SCALE + (row - lb) for sb, row, lb in zip(blocks(s), rows, blocks(lse3))],
                axis=0)
            if isinstance(d, int) and d == 0:
                x = jnp.where(jnp.logical_not(below()) | diagonal(), x, NEG)
            p = jnp.exp(x)
            dp = lax.dot_general(do, v, NT, preferred_element_type=F32)
            ds = (p * (dp - dl3) * SCALE).astype(BF16)
            dq = jnp.dot(ds, k, preferred_element_type=F32)
            if isinstance(d, int):
                dq_acc[h] = dq
            else:
                dq_acc[h] += dq

    def diagonal():
        return (lax.broadcasted_iota(jnp.int32, (ROWS, ROWS), 0)
                == lax.broadcasted_iota(jnp.int32, (ROWS, ROWS), 1))

    forward_units(middle_units, 2)

    @pl.when(first)
    def _():
        relay_units(own_unit[:3], 0)
        for d in range(1, 3):
            relay_units(mate_unit[:3], d)
        relay_units(own_unit[:3], 1)

    key_side(0)
    query_side(0)

    def chain_step(d, _):
        @pl.when(c + d <= RANKS - 1)
        def _():
            for u in late_units:
                do_copy(d - 1, u).wait_recv()
            de_copy(d - 1).wait_recv()

        @pl.when(jnp.logical_and(d == REACH - 1, c + d <= RANKS - 1))
        def _():
            for u in middle_units:
                do_copy(d - 1, u).wait_recv()

        send_units(middle_units, d, d == REACH - 1)
        send_units(late_units, d, True)
        send_delta(d, True)

        @pl.when(first)
        def _():
            relay_units([mate_unit[3], own_unit[3]], d - 1)
            relay_delta(d - 1)

        key_side(d)
        return 0

    last = REACH - 1

    @pl.when(c + REACH <= RANKS - 1)
    def _():
        q_copy(last).wait_recv()
        l_copy(last).wait_recv()
        for u in early_units:
            do_copy(last, u).wait_recv()

    lax.fori_loop(1, REACH, chain_step, 0)

    @pl.when(c + REACH <= RANKS - 1)
    def _():
        for u in middle_units + late_units:
            do_copy(last, u).wait_recv()
        de_copy(last).wait_recv()

    @pl.when(first)
    def _():
        relay_units(mate_unit[:3], 3)
        relay_units(own_unit[:3], 2)
        relay_units(own_unit[:3], 3)
        relay_units([mate_unit[3], own_unit[3]], 3)
        relay_delta(3)

    key_side(jnp.int32(REACH))

    part[:, 0:HEAD] = dk_acc[...].astype(BF16)
    part[:, HEAD:WIDE] = dv_acc[...].astype(BF16)

    def send(step):
        to = (t + step) % 8
        return remote(
            part.at[pl.ds(pl.multiple_of(to * PART, PART), PART)], land.at[step],
            r_ss.at[step], r_rs.at[step], (c, to))

    for step in range(1, 8):
        send(step).start()

    @pl.when(c - REACH >= 0)
    def _():
        kv_copy(last).wait_recv()

    def query_step(d, _):
        query_side(d)
        return 0

    lax.fori_loop(1, REACH + 1, query_step, 0)
    for h in range(2):
        dq_out[h] = dq_acc[h].astype(BF16)

    totals = [jnp.zeros((PART, WIDE), F32), jnp.zeros((PART, WIDE), F32)]
    for step in range(8):
        if step == 0:
            got = part[pl.ds(pl.multiple_of(t * PART, PART), PART), :].astype(F32)
        else:
            send(step).wait_recv()
            got = land[step].astype(F32)
        w1 = (((t + 8 - step) % 8) // 4).astype(F32)
        totals[0] = totals[0] + got * (1.0 - w1)
        totals[1] = totals[1] + got * w1
    for g in range(2):
        dkv_out[g] = totals[g].astype(BF16)

    for step in range(1, 8):
        send(step).wait_send()
    for cp in (g_up_a, g_up_b, g_dn_a, g_dn_b, *g_up_f, *g_dn_f, *w_sends, *s_sends):
        cp.wait_send()
    for s in range(4):
        x_copy(s).wait_send()
    for d in range(REACH):
        @pl.when(jnp.logical_or(first, back_ok(d)))
        def _():
            q_copy(d).wait_send()
            l_copy(d).wait_send()
            de_copy(d).wait_send()
            for u in range(8):
                do_copy(d, u).wait_send()

        @pl.when(jnp.logical_or(final, fwd_ok(d)))
        def _():
            kv_copy(d).wait_send()


def per_device(queries, key_tensor, value_tensor, attn_output, lse, grad_output, out_proj, block_doc):
    group = lax.axis_index("tp") // 4
    q2 = queries.reshape(ROWS, WIDE)
    o2 = attn_output.reshape(ROWS, WIDE)
    kv = jnp.concatenate(
        [
            lax.dynamic_index_in_dim(key_tensor, group, 1, keepdims=False),
            lax.dynamic_index_in_dim(value_tensor, group, 1, keepdims=False),
        ],
        axis=1,
    )
    vmem = pl.BlockSpec(memory_space=pltpu.VMEM)
    hbm = pl.BlockSpec(memory_space=pltpu.HBM)
    smem = pl.BlockSpec(memory_space=pltpu.SMEM)
    dma = pltpu.SemaphoreType.DMA
    span = REACH + 1
    dq, dkv = pl.pallas_call(
        fused_kernel,
        out_shape=(
            jax.ShapeDtypeStruct((2, ROWS, HEAD), BF16),
            jax.ShapeDtypeStruct((2, PART, WIDE), BF16),
        ),
        in_specs=[smem] + [hbm] * 6,
        out_specs=(vmem, vmem),
        scratch_shapes=[
            pltpu.VMEM((span, ROWS, WIDE), BF16),
            pltpu.VMEM((span, ROWS, WIDE), BF16),
            pltpu.VMEM((span, 2, ROWS), F32),
            pltpu.VMEM((span, 8, PART, WIDE), BF16),
            pltpu.VMEM((span, 2, ROWS), F32),
            pltpu.VMEM((ROWS, WIDE), BF16),
            pltpu.VMEM((2, ROWS, HEAD), F32),
            pltpu.VMEM((2, ROWS, HEAD), F32),
            pltpu.VMEM((WIDE, D), BF16),
            pltpu.VMEM((WIDE, D), BF16),
            pltpu.VMEM((4 * PART, D), BF16),
            pltpu.VMEM((4, PART, WIDE), BF16),
            pltpu.VMEM((4 * PART, WIDE), F32),
            pltpu.VMEM((PART, WIDE), F32),
            pltpu.VMEM((ROWS, HEAD), F32),
            pltpu.VMEM((ROWS, HEAD), F32),
            pltpu.VMEM((2, ROWS, HEAD), F32),
            pltpu.VMEM((ROWS, WIDE), BF16),
            pltpu.VMEM((8, PART, WIDE), BF16),
            dma((6,)), dma((8,)), dma((8,)), dma((4,)), dma((4,)), dma((4,)), dma((4,)),
            dma((4,)), dma((4,)), dma((4,)), dma((4,)), dma((4,)), dma((4,)),
            dma((4,)), dma((4,)), dma((4, 8)), dma((4, 8)), dma((4,)), dma((4,)),
            dma((8,)), dma((8,)), pltpu.SemaphoreType.REGULAR,
            pltpu.VMEM((REACH, ROWS, WIDE), BF16),
            pltpu.VMEM((REACH, 2, ROWS), F32),
            pltpu.VMEM((REACH, ROWS, WIDE), BF16),
            pltpu.VMEM((REACH, 8, PART, WIDE), BF16),
            pltpu.VMEM((REACH, 2, ROWS), F32),
            dma((4,)), dma((4,)), dma((4,)), dma((4, 8)), dma((4,)),
        ],
        compiler_params=pltpu.CompilerParams(
            collective_id=0, has_side_effects=True, vmem_limit_bytes=67043328 - 720 * 1024),
        name="attention_backward",
    )(block_doc, q2, kv, lse, o2, grad_output, out_proj)
    grad_query = jnp.transpose(dq, (1, 0, 2))
    grad_key = jnp.transpose(dkv[:, :, :HEAD], (1, 0, 2))
    grad_value = jnp.transpose(dkv[:, :, HEAD:], (1, 0, 2))
    return grad_query, grad_key, grad_value


def solution(mesh):
    placed = (
        P("ctx", "tp", None),
        P("ctx", None, None),
        P("ctx", None, None),
        P("ctx", "tp", None),
        P("tp", "ctx"),
        P(("ctx", "tp"), None),
        P("tp", None),
        P(),
    )
    return jax.shard_map(
        per_device,
        mesh=mesh,
        in_specs=placed,
        out_specs=(
            P("ctx", "tp", None),
            P(("ctx", "tp"), None, None),
            P(("ctx", "tp"), None, None),
        ),
        check_vma=False,
    )
```

time: 119 us -> 83.8 us (0.70)
  the two profiles are of different devices: /device:TPU:97 before, /device:TPU:8 now
where the time goes in v2:
time: 83.8 us; the launch traced here: 83.5 us
  Pallas kernels  75 us (89%)
  local copies, waits for them, and re-layouts  7.09 us (8%)
    pallas_call x1, Pallas kernels, per_device(): pl.pallas_call(fused_kernel, out_shape=(jax.ShapeDtypeStruct((2, ROWS, HE...  75 us
    unnamed x5, local copies, waits for them, and re-layouts  3.09 us
    reshape x1, local copies, waits for them, and re-layouts, per_device(): o2 = attn_output.reshape(ROWS, WIDE)  1.81 us

profile of v2, /device:TPU:8, one launch (start us, length us, event | category | flops | bytes accessed | tf_op | source)
XLA Modules:
  0.0 83.5 jit_solution(17266329206894215911)
XLA Ops:
  0.6 1.4 %constant_dynamic-slice_fusion = (bf16[384,1,128]{2,1,0:T(2,128)(2,1)S(1)}, bf16[384,1,128]{2,1,0:T(2,128)(2,1)S(1)}) fusion(bf16[384,2,128]{2,1,0:T(2,128)(2,1)} %param.10, s32[]{:T(128)S(6)} %select_n.11, bf16[384,2,128]{2,1,0:T(2,128)(2,1)} %param.9), kind=kLoop, calls=%fused_computation.7 | loop fusion | bytes 393220 | tf_op jit(solution)/shard_map/jit(dynamic_index_in_dim)/dynamic_slice | solution.py:627
  2.1 0.7 pad_maximum_fusion.kv_in
  2.8 1.8 %copy_bitcast_fusion = (bf16[384,256]{1,0:T(8,128)(2,1)}, bf16[384,256]{1,0:T(8,128)(2,1)}) fusion(bf16[48,8,2,128]{3,2,1,0:T(2,128)(2,1)} %bitcast.20, bf16[48,8,2,128]{3,2,1,0:T(2,128)(2,1)} %bitcast.21), kind=kLoop, calls=%fused_computation | loop fusion | bytes 786432 | tf_op jit(solution)/shard_map/reshape | solution.py:623
  4.6 75.0 %attention_backward.1 = (bf16[2,384,128]{2,1,0:T(8,128)(2,1)}, bf16[2,48,256]{2,1,0:T(8,128)(2,1)}) custom-call(s32[384]{0:T(512)} %docs.1, bf16[384,256]{1,0:T(8,128)(2,1)} %get-tuple-element.18.q_in, bf16[384,256]{1,0:T(8,128)(2,1)} %pad_maximum_fusion.kv_in, f32[2,384]{1,0:T(2,128)} %lse_in.1, bf16[384,256]{1,0:T(8,128)(2,1)} %get-tuple-element.17.o_hbm, ...), custom_call_target="tpu_custom_call" | custom-call | tf_op jit(solution)/shard_map/attention_backward/pallas_call | solution.py:636
  79.7 1.8 %copy.16 = bf16[384,2,128]{2,1,0:T(2,128)(2,1)} copy(bf16[384,2,128]{2,0,1:T(8,128)(2,1)} %bitcast.19) | data formatting | bytes 393216
  81.5 0.8 slice_bitcast_fusion
  82.2 0.6 copy.18
  82.9 0.6 copy.17
  (2 shorter events, 0.0 us)

commit v3 on v2

--- a/solution.py
+++ b/solution.py
@@ -30,7 +30,7 @@
 
 
 def fused_kernel(
-    docs, q_in, kv_in, lse_in, o_hbm, g_hbm, w_hbm,
+    docs, q_in, k_in, v_in, lse_in, o_hbm, g_hbm, w_hbm,
     dq_out, dkv_out,
     qw, kvw, lsew, dow, delw, o_in, lsec, delc,
     wmine, woth, gbuf, xsend, acc_t, acc_m, dk_acc, dv_acc, dq_acc, part, land,
@@ -152,8 +152,7 @@
         return remote(src, lsew.at[d + 1], l_ss.at[d], l_rs.at[d], prev)
 
     def kv_copy(d):
-        src = kv_in if d == 0 else kvw.at[d]
-        return remote(src, kvw.at[d + 1], kv_ss.at[d], kv_rs.at[d], nxt)
+        return remote(kvw.at[d], kvw.at[d + 1], kv_ss.at[d], kv_rs.at[d], nxt)
 
     def do_copy(d, u):
         return remote(dow.at[d, u], dow.at[d + 1, u], do_ss.at[d, u], do_rs.at[d, u], prev)
@@ -168,7 +167,7 @@
         return lse_in if isinstance(d, int) and d == 0 else lsew.at[d]
 
     def kv_src(d):
-        return kv_in if isinstance(d, int) and d == 0 else kvw.at[d]
+        return kvw.at[d]
 
     def send_q(d, when):
         ok = jnp.logical_and(when, back_ok(d))
@@ -243,20 +242,21 @@
         remote(rkv.at[d], kvw.at[d + 1], kv_ss.at[d], kv_rs.at[d], on_to).start()
 
     send_q(0, True)
-    send_kv(0, True)
 
     w_loc = pltpu.make_async_copy(w_hbm, wmine, loc_sem.at[0])
     g_loc = pltpu.make_async_copy(g_hbm, gbuf.at[pl.ds(0, PART), :], loc_sem.at[1])
+    group = pl.ds(pl.multiple_of(xlo * HEAD, HEAD), HEAD)
     locals_ = [
         pltpu.make_async_copy(q_in, qw.at[0], loc_sem.at[2]),
-        pltpu.make_async_copy(kv_in, kvw.at[0], loc_sem.at[3]),
+        pltpu.make_async_copy(k_in.at[:, group], kvw.at[0, :, pl.ds(0, HEAD)], loc_sem.at[3]),
+        pltpu.make_async_copy(v_in.at[:, group], kvw.at[0, :, pl.ds(HEAD, HEAD)], loc_sem.at[6]),
         pltpu.make_async_copy(lse_in, lsew.at[0], loc_sem.at[4]),
         pltpu.make_async_copy(o_hbm, o_in, loc_sem.at[5]),
     ]
+    for cp in locals_:
+        cp.start()
     w_loc.start()
     g_loc.start()
-    for cp in locals_:
-        cp.start()
     for d in range(1, REACH + 1):
         @pl.when(c + d > RANKS - 1)
         def _():
@@ -311,10 +311,11 @@
 
         send_kv(d, when)
 
+    for cp in locals_:
+        cp.wait()
+    send_kv(0, True)
     w_loc.wait()
     g_loc.wait()
-    for cp in locals_:
-        cp.wait()
     mine(0, 1)
     send_units(early_units[:1], 0, True)
 
@@ -364,15 +365,6 @@
     for i in range(2):
         s_sends[i].wait_recv()
     acc_t[0:3 * PART, :] = partial_product(0, 3, woth, even, SUB)
-
-    @pl.when(first)
-    def _():
-        pl.semaphore_wait(ready, 1)
-        for d in range(REACH):
-            for one, two in zip(relay_q_in(d), relay_q(d)):
-                one.wait_recv()
-                two.start()
-        relay_units(mate_unit[:3], 0)
 
     forward_units(early_units, 1)
     forward_q(1, q_over(1))
@@ -386,6 +378,20 @@
     forward_q(2, q_over(2))
     for i in range(2, 4):
         s_sends[i].wait_recv()
+
+    def hand_on_q(d):
+        for one, two in zip(relay_q_in(d), relay_q(d)):
+            one.wait_recv()
+            two.start()
+
+    @pl.when(first)
+    def _():
+        pl.semaphore_wait(ready, 1)
+        hand_on_q(0)
+        relay_units(mate_unit[:3], 0)
+        for d in range(1, REACH):
+            hand_on_q(d)
+
     out = (acc_t[0:3 * PART, :] + partial_product(0, 3, woth, odd, SUB)).astype(BF16)
     for s in range(3):
         xsend[s] = out[s * PART:(s + 1) * PART]
@@ -419,8 +425,6 @@
 
     forward_units(early_units, 3)
     forward_q(3, q_over(3))
-    for d in range(1, REACH):
-        forward_kv(d, kv_over(d))
 
     lane_blk = lax.broadcasted_iota(jnp.int32, (1, ROWS), 1) // HEAD
 
@@ -497,7 +501,7 @@
         return (lax.broadcasted_iota(jnp.int32, (ROWS, ROWS), 0)
                 == lax.broadcasted_iota(jnp.int32, (ROWS, ROWS), 1))
 
-    forward_units(middle_units, 2)
+    key_side(0)
 
     @pl.when(first)
     def _():
@@ -506,8 +510,6 @@
             relay_units(mate_unit[:3], d)
         relay_units(own_unit[:3], 1)
 
-    key_side(0)
-    query_side(0)
 
     def chain_step(d, _):
         @pl.when(c + d <= RANKS - 1)
@@ -516,14 +518,15 @@
                 do_copy(d - 1, u).wait_recv()
             de_copy(d - 1).wait_recv()
 
-        @pl.when(jnp.logical_and(d == REACH - 1, c + d <= RANKS - 1))
-        def _():
-            for u in middle_units:
-                do_copy(d - 1, u).wait_recv()
-
-        send_units(middle_units, d, d == REACH - 1)
         send_units(late_units, d, True)
         send_delta(d, True)
+
+        @pl.when(jnp.logical_and(d < REACH - 1, c + d + 1 <= RANKS - 1))
+        def _():
+            for u in middle_units:
+                do_copy(d, u).wait_recv()
+
+        send_units(middle_units, d + 1, d < REACH - 1)
 
         @pl.when(first)
         def _():
@@ -542,7 +545,9 @@
         for u in early_units:
             do_copy(last, u).wait_recv()
 
-    lax.fori_loop(1, REACH, chain_step, 0)
+    chain_step(jnp.int32(1), 0)
+    query_side(0)
+    lax.fori_loop(2, REACH, chain_step, 0)
 
     @pl.when(c + REACH <= RANKS - 1)
     def _():
@@ -571,6 +576,9 @@
 
     for step in range(1, 8):
         send(step).start()
+
+    for d in range(1, REACH):
+        forward_kv(d, kv_over(d))
 
     @pl.when(c - REACH >= 0)
     def _():
@@ -618,16 +626,10 @@
 
 
 def per_device(queries, key_tensor, value_tensor, attn_output, lse, grad_output, out_proj, block_doc):
-    group = lax.axis_index("tp") // 4
     q2 = queries.reshape(ROWS, WIDE)
+    k2 = key_tensor.reshape(ROWS, WIDE)
+    v2 = value_tensor.reshape(ROWS, WIDE)
     o2 = attn_output.reshape(ROWS, WIDE)
-    kv = jnp.concatenate(
-        [
-            lax.dynamic_index_in_dim(key_tensor, group, 1, keepdims=False),
-            lax.dynamic_index_in_dim(value_tensor, group, 1, keepdims=False),
-        ],
-        axis=1,
-    )
     vmem = pl.BlockSpec(memory_space=pltpu.VMEM)
     hbm = pl.BlockSpec(memory_space=pltpu.HBM)
     smem = pl.BlockSpec(memory_space=pltpu.SMEM)
@@ -639,7 +641,7 @@
             jax.ShapeDtypeStruct((2, ROWS, HEAD), BF16),
             jax.ShapeDtypeStruct((2, PART, WIDE), BF16),
         ),
-        in_specs=[smem] + [hbm] * 6,
+        in_specs=[smem] + [hbm] * 7,
         out_specs=(vmem, vmem),
         scratch_shapes=[
             pltpu.VMEM((span, ROWS, WIDE), BF16),
@@ -661,7 +663,7 @@
             pltpu.VMEM((2, ROWS, HEAD), F32),
             pltpu.VMEM((ROWS, WIDE), BF16),
             pltpu.VMEM((8, PART, WIDE), BF16),
-            dma((6,)), dma((8,)), dma((8,)), dma((4,)), dma((4,)), dma((4,)), dma((4,)),
+            dma((7,)), dma((8,)), dma((8,)), dma((4,)), dma((4,)), dma((4,)), dma((4,)),
             dma((4,)), dma((4,)), dma((4,)), dma((4,)), dma((4,)), dma((4,)),
             dma((4,)), dma((4,)), dma((4, 8)), dma((4, 8)), dma((4,)), dma((4,)),
             dma((8,)), dma((8,)), pltpu.SemaphoreType.REGULAR,
@@ -673,9 +675,9 @@
             dma((4,)), dma((4,)), dma((4,)), dma((4, 8)), dma((4,)),
         ],
         compiler_params=pltpu.CompilerParams(
-            collective_id=0, has_side_effects=True, vmem_limit_bytes=67043328 - 720 * 1024),
+            collective_id=0, has_side_effects=True, vmem_limit_bytes=53 << 20),
         name="attention_backward",
-    )(block_doc, q2, kv, lse, o2, grad_output, out_proj)
+    )(block_doc, q2, k2, v2, lse, o2, grad_output, out_proj)
     grad_query = jnp.transpose(dq, (1, 0, 2))
     grad_key = jnp.transpose(dkv[:, :, :HEAD], (1, 0, 2))
     grad_value = jnp.transpose(dkv[:, :, HEAD:], (1, 0, 2))

time: 83.8 us -> 80.6 us (0.962)
  the two profiles are of different devices: /device:TPU:8 before, /device:TPU:929 now
where the time goes in v3:
time: 80.6 us; the launch traced here: 80.4 us
  Pallas kernels  73.4 us (91%)
  local copies, waits for them, and re-layouts  6.34 us (8%)
    pallas_call x1, Pallas kernels, per_device(): pl.pallas_call(fused_kernel, out_shape=(jax.ShapeDtypeStruct((2, ROWS, HE...  73.4 us
    unnamed x7, local copies, waits for them, and re-layouts  3.5 us
    reshape x1, local copies, waits for them, and re-layouts, per_device(): o2 = attn_output.reshape(ROWS, WIDE)  1.75 us

profile of v3, /device:TPU:929, one launch (start us, length us, event | category | flops | bytes accessed | tf_op | source)
XLA Modules:
  0.0 80.4 jit_solution(11792104613147965605)
XLA Ops:
  0.6 1.1 %copy_bitcast_fusion.2 = (bf16[384,256]{1,0:T(8,128)(2,1)S(1)}, bf16[384,256]{1,0:T(8,128)(2,1)S(1)}) fusion(bf16[48,8,2,128]{3,2,1,0:T(2,128)(2,1)} %bitcast.18, bf16[48,8,2,128]{3,2,1,0:T(2,128)(2,1)} %bitcast.19), kind=kLoop, calls=%fused_computation.2 | loop fusion | bytes 786432 | tf_op jit(solution)/shard_map/reshape | solution.py:630
  1.7 1.8 %copy_bitcast_fusion = (bf16[384,256]{1,0:T(8,128)(2,1)}, bf16[384,256]{1,0:T(8,128)(2,1)S(1)}) fusion(bf16[48,8,2,128]{3,2,1,0:T(2,128)(2,1)} %bitcast.20, bf16[48,8,2,128]{3,2,1,0:T(2,128)(2,1)} %bitcast.21), kind=kLoop, calls=%fused_computation | loop fusion | bytes 786432 | tf_op jit(solution)/shard_map/reshape | solution.py:632
  3.5 0.0 copy-start
  3.5 0.7 copy-done
  4.1 0.0 copy-start.1
  4.1 0.7 copy-done.1
  4.8 73.4 %attention_backward.1 = (bf16[2,384,128]{2,1,0:T(8,128)(2,1)S(1)}, bf16[2,48,256]{2,1,0:T(8,128)(2,1)S(1)}) custom-call(s32[384]{0:T(512)S(1)} %copy-done.1, bf16[384,256]{1,0:T(8,128)(2,1)S(1)} %get-tuple-element.15.q_in, bf16[384,256]{1,0:T(8,128)(2,1)S(1)} %get-tuple-element.14.k_in, bf16[384,256]{1,0:T(8,128)(2,1)S(1)} %get-tuple-element.13.v_in, ...), custom_call_target="tpu_custom_call" | custom-call | tf_op jit(solution)/shard_map/attention_backward/pallas_call | solution.py:638
  78.2 0.9 %copy.11 = bf16[384,2,128]{2,1,0:T(2,128)(2,1)} copy(bf16[384,2,128]{2,0,1:T(8,128)(2,1)S(1)} %bitcast.17) | data formatting | bytes 393216
  79.1 0.6 copy.13
  79.7 0.6 copy.12
  (1 shorter events, 0.0 us)
Async XLA Ops:
  3.5 0.7 copy-start
  4.1 0.7 copy-start.1
